TPU v7x, 256 devices: a whole 4x4x8 slice. The times are simulated.
256 devices in a mesh: dp: 32 (over y, z), cent: 8 (over x, core).
Axes of the slice: x: 4, y: 4, z: 8, core: 2. Of those that a mesh axis runs over, the one named last changes fastest.
Arguments:
- embeddings: bfloat16 [16384, 768], P('dp'), may hold values from -400 to 400, as said below
- centroids: bfloat16 [16384, 768], P('cent'), may hold values from -400 to 400, as said below
Outputs:
- new_centroids: float32 [16384, 768], P(('cent', 'dp'))
Inputs may be any that keep to these rules, and one draw needn't show every extreme that they name: `embeddings`: finite real values. `centroids`: finite real values.
All inputs are finite; a program needn't handle non-finite values.
Results may differ from a plain program's by a relative error of at most 0.0038.
Values sent between devices are 32-bit elements; how exact they have to be, the bound alone decides.
A program may use at most 64 MiB of HBM per device.

v0:
```python
import jax
import jax.numpy as jnp
from jax import lax
from jax.sharding import PartitionSpec as P

FEATURE_DIM = 768
ROUNDS = 2
entropy_regularizer = 0.05


def normalize(values):
    wide = values.astype(jnp.float32)
    meansq = jnp.mean(wide * wide, axis=-1, keepdims=True)
    return (wide * lax.rsqrt(meansq + 1e-06)).astype(jnp.bfloat16)


def row_update(boltzmann_affinity, column_factor):
    partial_rows = jnp.dot(boltzmann_affinity, column_factor, precision=lax.Precision.HIGHEST)
    totals = lax.psum(partial_rows, "cent")
    return 1.0 / totals


def shards(embeddings, centroids):
    normed = normalize(embeddings)
    cent_normed = normalize(centroids)
    cosine_matches = lax.dot_general(
        normed, cent_normed, (((1,), (1,)), ((), ())), preferred_element_type=jnp.float32
    )
    boltzmann_affinity = jnp.exp(cosine_matches * (1.0 / (FEATURE_DIM * entropy_regularizer)))
    local_cents = centroids.shape[0]
    row_count = embeddings.shape[0] * lax.axis_size("dp")
    cent_count = local_cents * lax.axis_size("cent")
    balance_ratio = row_count / cent_count
    column_factor = jnp.ones((local_cents,), jnp.float32)
    for sweep in range(ROUNDS):
        row_weight = row_update(boltzmann_affinity, column_factor)
        partial_cols = jnp.dot(row_weight, boltzmann_affinity, precision=lax.Precision.HIGHEST)
        column_factor = balance_ratio / lax.psum(partial_cols, "dp")
    row_weight = row_update(boltzmann_affinity, column_factor)
    transport = (row_weight[:, None] * boltzmann_affinity * column_factor[None, :]).astype(
        jnp.bfloat16
    )
    col_mass = jnp.sum(transport, axis=0, dtype=jnp.float32)
    own_rows = local_cents // lax.axis_size("dp")
    holder_position = lax.axis_index("dp")
    weighted = lax.dot_general(
        transport, normed, (((0,), (0,)), ((), ())), preferred_element_type=jnp.float32
    )
    weighted, col_mass = lax.psum((weighted, col_mass), "dp")
    weighted = lax.dynamic_slice_in_dim(weighted, holder_position * own_rows, own_rows, 0)
    col_mass = lax.dynamic_slice_in_dim(col_mass, holder_position * own_rows, own_rows, 0)
    return weighted / col_mass[:, None]


def solution(mesh):
    in_specs = (P("dp", None), P("cent", None))
    out_specs = P(("cent", "dp"), None)
    return jax.shard_map(shards, mesh=mesh, in_specs=in_specs, out_specs=out_specs, check_vma=False)
```

profile of v0, /device:TPU:1, one launch (start us, length us, event | category | flops | bytes accessed | tf_op | source)
XLA Modules:
  0.0 423.9 jit_solution(16495555627973379805)
XLA Ops:
  6.5 0.0 all-reduce.2.cloned.1.call-start
  6.5 1.4 fusion.4
  7.9 2.6 fusion
  10.5 4.1 multiply_exponential_fusion
  14.6 0.0 copy-start
  14.6 1.9 copy-done
  16.6 3.6 fusion.9
  20.2 15.0 %psum.49 = f32[512]{0:T(512)S(1)} all-reduce(f32[512]{0:T(512)S(1)} %bitcast.25), channel_id=1, replica_groups=mesh['dp'=32,'cent'=8] {'cent'}, use_global_device_ids=true, to_apply=%region_2.0 | all-reduce | flops 512 | bytes 4096 | tf_op jit(solution)/shard_map/psum | solution.py:19
  35.2 4.3 %fusion.12 = f32[1,2048]{1,0:T(1,128)S(1)} fusion(f32[512,1]{0,1:T(1,128)S(1)} %bitcast.22, f32[512,2048]{1,0:T(8,128)} %copy-done), kind=kOutput, calls=%fused_computation.24 | convolution fusion | flops 12582912 | bytes 4204544 | tf_op jit(solution)/shard_map/dot_general | solution.py:37
  39.4 63.4 %psum.50 = f32[2048]{0:T(1024)S(1)} all-reduce(f32[2048]{0:T(1024)S(1)} %bitcast.19), channel_id=1, replica_groups=mesh['dp'=32,'cent'=8] {'dp'}, use_global_device_ids=true, to_apply=%region_3.0 | all-reduce | flops 2048 | bytes 16384 | tf_op jit(solution)/shard_map/psum | solution.py:38
  102.9 5.8 %fusion.13 = f32[1,512]{1,0:T(1,128)S(1)} fusion(f32[512,2048]{1,0:T(8,128)} %copy-done, f32[2048,1]{0,1:T(1,128)S(1)} %bitcast.20), kind=kOutput, calls=%fused_computation.25 | convolution fusion | flops 12582912 | bytes 4204544 | tf_op jit(solution)/shard_map/dot_general | solution.py:18
  108.6 28.6 %psum.51 = f32[512]{0:T(512)S(1)} all-reduce(f32[512]{0:T(512)S(1)} %bitcast.23), channel_id=1, replica_groups=mesh['dp'=32,'cent'=8] {'cent'}, use_global_device_ids=true, to_apply=%region_4.0 | all-reduce | flops 512 | bytes 4096 | tf_op jit(solution)/shard_map/psum | solution.py:19
  137.2 4.3 %fusion.14 = f32[1,2048]{1,0:T(1,128)S(1)} fusion(f32[512,1]{0,1:T(1,128)S(1)} %bitcast.24, f32[512,2048]{1,0:T(8,128)} %copy-done), kind=kOutput, calls=%fused_computation.26 | convolution fusion | flops 12582912 | bytes 4204544 | tf_op jit(solution)/shard_map/dot_general | solution.py:37
  141.6 57.2 %psum.52 = f32[2048]{0:T(1024)S(1)} all-reduce(f32[2048]{0:T(1024)S(1)} %bitcast.21), channel_id=1, replica_groups=mesh['dp'=32,'cent'=8] {'dp'}, use_global_device_ids=true, to_apply=%region_5.0 | all-reduce | flops 2048 | bytes 16384 | tf_op jit(solution)/shard_map/psum | solution.py:38
  198.8 5.8 %fusion.15 = f32[1,512]{1,0:T(1,128)S(1)} fusion(f32[512,2048]{1,0:T(8,128)} %copy-done, f32[2048,1]{0,1:T(1,128)S(1)} %bitcast.18), kind=kOutput, calls=%fused_computation.27 | convolution fusion | flops 12582912 | bytes 4204544 | tf_op jit(solution)/shard_map/dot_general | solution.py:18
  204.6 25.8 %psum.53 = f32[512]{0:T(512)S(1)} all-reduce(f32[512]{0:T(512)S(1)} %bitcast.26), channel_id=1, replica_groups=mesh['dp'=32,'cent'=8] {'cent'}, use_global_device_ids=true, to_apply=%region_6.0 | all-reduce | flops 512 | bytes 4096 | tf_op jit(solution)/shard_map/psum | solution.py:19
  230.4 0.0 copy-done.1
  230.4 6.8 %fusion.6 = f32[2048,768]{1,0:T(8,128)} fusion(bf16[512,768]{1,0:T(8,128)(2,1)S(1)} %copy-done.1, f32[512]{0:T(512)S(1)} %add_rsqrt_fusion.1, f32[512,2048]{1,0:T(8,128)} %copy-done, f32[2048]{0:T(1024)S(1)} %broadcast_divide_fusion.1, f32[512]{0:T(512)S(1)} %broadcast_divide_fusion.2), kind=kOutput, calls=%fused_computation.12 | convolution fusion | flops 1614938112 | bytes 11284480 | tf_op jit(solution)/shard_map/dot_general | solution.py:46
  237.3 0.0 all-reduce.2.cloned.1.call-update
  237.3 2.7 convert_reduce_fusion
  240.0 62.2 %psum.55 = f32[2048]{0:T(1024)S(1)} all-reduce(f32[2048]{0:T(1024)S(1)} %convert_reduce_fusion), channel_id=1, replica_groups=mesh['dp'=32,'cent'=8] {'dp'}, use_global_device_ids=true, to_apply=%region_9.0 | all-reduce | flops 2048 | bytes 16384 | tf_op jit(solution)/shard_map/psum | solution.py:49
  302.2 0.1 dynamic_slice.7
  302.3 113.1 %all-reduce.2.cloned.1.call-done = f32[2048,768]{1,0:T(8,128)} async-done(((f32[2048,768]{1,0:T(8,128)}), f32[2048,768]{1,0:T(8,128)}) %all-reduce.2.cloned.1.call-update) | async-done | bytes 6291472 | tf_op jit(solution)/shard_map/psum | solution.py:49
  415.3 1.7 dynamic-slice_divide_fusion
  (8 shorter events, 0.0 us)
Async XLA Ops:
  6.5 408.8 %all-reduce.2.cloned.1.call-start = ((), (), s32[]{:S(2)}) async-start(), calls=%async_computation | async-start | bytes 12582912 | tf_op jit(solution)/shard_map/psum | solution.py:49
  14.6 2.0 copy-start
  137.2 93.2 %copy-start.1 = (bf16[512,768]{1,0:T(8,128)(2,1)S(1)}, bf16[512,768]{1,0:T(8,128)(2,1)}, u32[]{:S(2)}) copy-start(bf16[512,768]{1,0:T(8,128)(2,1)} %param.2) | copy-start | bytes 2359300
Sparse Core Ops, SparseCore 0:
  237.4 177.8 all-reduce.1
where the time goes:
time: 424 us
  blocking collectives  252 us (59%)
  waiting for transfers between devices  113 us (27%)
  matrix products  34.7 us (8%)
  between operations  13.5 us (3%)
  other arithmetic  8.35 us (2%)
    psum x2, blocking collectives, shards(): column_factor = balance_ratio / lax.psum(partial_cols, 'dp')  121 us
    psum x1, waiting for transfers between devices, shards(): weighted, col_mass = lax.psum((weighted, col_mass), 'dp')  113 us
    psum x3, blocking collectives, row_update(): totals = lax.psum(partial_rows, 'cent')  69.4 us
    psum x1, blocking collectives, shards(): weighted, col_mass = lax.psum((weighted, col_mass), 'dp')  62.2 us
    dot_general x3, matrix products, row_update(): jnp.dot(boltzmann_affinity, column_factor, precision=lax.Precision.HIGHEST)  15.1 us
    dot_general x2, matrix products, shards(): jnp.dot(row_weight, boltzmann_affinity, precision=lax.Precision.HIGHEST)  8.61 us
  transfers between devices with their start and end apart: 1, of which 1 were waited for; matrix products, arithmetic and copies ran while one was open for 1% of the time, Pallas kernels for 0%

commit v1 on v0

--- a/solution.py
+++ b/solution.py
@@ -16,7 +16,9 @@
 
 def row_update(boltzmann_affinity, column_factor):
     partial_rows = jnp.dot(boltzmann_affinity, column_factor, precision=lax.Precision.HIGHEST)
-    totals = lax.psum(partial_rows, "cent")
+    totals = partial_rows
+    for hop in (1, 2, 4):
+        totals = totals + lax.ppermute(totals, "cent", [(dev, dev ^ hop) for dev in range(8)])
     return 1.0 / totals
 
 

time: 424 us -> 409 us (0.965)
  blocking collectives: 252 us -> 181 us
  starting transfers between devices: 0.01 us -> 45.4 us
  waiting for transfers between devices: 113 us -> 131 us
  matrix products: 34.7 us -> 28.4 us
    psum x3 -> x0, blocking collectives: 69.4 us -> none  [row_update(): totals = lax.psum(partial_rows, 'cent')]
    ppermute x0 -> x9, starting transfers between devices: none -> 45.4 us  [row_update(): lax.ppermute(totals, 'cent', [(dev, dev ^ hop) for dev in range(8)])]
    ppermute x0 -> x9, waiting for transfers between devices: none -> 12.7 us  [row_update(): lax.ppermute(totals, 'cent', [(dev, dev ^ hop) for dev in range(8)])]
    psum x1, waiting for transfers between devices: 113 us -> 119 us  [shards(): weighted, col_mass = lax.psum((weighted, col_mass), 'dp')]
    dot_general x2, matrix products: 8.61 us -> 4.15 us  [shards(): jnp.dot(row_weight, boltzmann_affinity, precision=lax.Precision.HIGHEST)]
  transfers between devices with their start and end apart: 1 -> 10, of which waited for: 1 -> 10; matrix products, arithmetic and copies ran while one was open for 1% -> 1% of each run, Pallas kernels for 0% -> 0%
where the time goes in v1:
time: 409 us; the launch traced here: 408 us
  blocking collectives  181 us (44%)
  waiting for transfers between devices  131 us (32%)
  starting transfers between devices  45.4 us (11%)
  matrix products  28.4 us (7%)
  between operations  13.5 us (3%)
  other arithmetic  8.37 us (2%)
    psum x2, blocking collectives, shards(): column_factor = balance_ratio / lax.psum(partial_cols, 'dp')  120 us
    psum x1, waiting for transfers between devices, shards(): weighted, col_mass = lax.psum((weighted, col_mass), 'dp')  119 us
    psum x1, blocking collectives, shards(): weighted, col_mass = lax.psum((weighted, col_mass), 'dp')  61 us
    ppermute x9, starting transfers between devices, row_update(): lax.ppermute(totals, 'cent', [(dev, dev ^ hop) for dev in range(8)])  45.4 us
    dot_general x3, matrix products, row_update(): jnp.dot(boltzmann_affinity, column_factor, precision=lax.Precision.HIGHEST)  15.4 us
    ppermute x9, waiting for transfers between devices, row_update(): lax.ppermute(totals, 'cent', [(dev, dev ^ hop) for dev in range(8)])  12.7 us
  transfers between devices with their start and end apart: 10, of which 10 were waited for; matrix products, arithmetic and copies ran while one was open for 1% of the time, Pallas kernels for 0%

profile of v1, /device:TPU:1, one launch (start us, length us, event | category | flops | bytes accessed | tf_op | source)
XLA Modules:
  0.0 408.3 jit_solution(7892061383444774427)
XLA Ops:
  6.5 1.4 fusion.4
  7.9 2.6 fusion
  10.5 4.1 %multiply_exponential_fusion = f32[512,2048]{1,0:T(8,128)S(1)} fusion(bf16[2048,768]{1,0:T(8,128)(2,1)} %param.3, f32[2048]{0:T(1024)S(1)} %add_rsqrt_fusion, bf16[512,768]{1,0:T(8,128)(2,1)} %param.2, f32[512]{0:T(512)S(1)} %add_rsqrt_fusion.1), kind=kOutput, calls=%fused_computation.6 | convolution fusion | flops 1617559552 | bytes 8136704 | tf_op jit(solution)/shard_map/dot_general | solution.py:28
  14.6 3.6 fusion.9
  18.2 3.2 collective-permute-start
  22.3 2.4 collective-permute-done.1
  25.8 2.9 collective-permute-done.2
  28.7 2.1 fusion.12
  30.8 63.4 %psum.28 = f32[2048]{0:T(1024)S(1)} all-reduce(f32[2048]{0:T(1024)S(1)} %bitcast.19), channel_id=1, replica_groups=mesh['dp'=32,'cent'=8] {'dp'}, use_global_device_ids=true, to_apply=%region_2.0 | all-reduce | flops 2048 | bytes 16384 | tf_op jit(solution)/shard_map/psum | solution.py:40
  94.1 5.9 %fusion.13 = f32[1,512]{1,0:T(1,128)S(1)} fusion(f32[512,2048]{1,0:T(8,128)} %copy-done, f32[2048,1]{0,1:T(1,128)S(1)} %bitcast.20), kind=kOutput, calls=%fused_computation.25 | convolution fusion | flops 12582912 | bytes 4204544 | tf_op jit(solution)/shard_map/dot_general | solution.py:18
  100.1 16.7 %collective-permute-start.3 = (f32[512]{0:T(512)S(1)}, f32[512]{0:T(512)S(1)}, u32[]{:S(2)}, u32[]{:S(2)}) collective-permute-start(f32[512]{0:T(512)S(1)} %bitcast.22), channel_id=1, source_target_pairs={{0,1},{1,0},{2,3},{3,2},{4,5},{5,4},{6,7},{7,6},{8,9},{9,8},{10,11... | collective-permute-start | bytes 6152 | tf_op jit(solution)/shard_map/ppermute | solution.py:21
  118.8 1.2 collective-permute-done.4
  120.0 2.7 collective-permute-start.5
  124.0 2.1 fusion.14
  126.1 56.7 %psum.29 = f32[2048]{0:T(1024)S(1)} all-reduce(f32[2048]{0:T(1024)S(1)} %bitcast.21), channel_id=1, replica_groups=mesh['dp'=32,'cent'=8] {'dp'}, use_global_device_ids=true, to_apply=%region_3.0 | all-reduce | flops 2048 | bytes 16384 | tf_op jit(solution)/shard_map/psum | solution.py:40
  182.8 5.9 %fusion.15 = f32[1,512]{1,0:T(1,128)S(1)} fusion(f32[512,2048]{1,0:T(8,128)} %copy-done, f32[2048,1]{0,1:T(1,128)S(1)} %bitcast.18), kind=kOutput, calls=%fused_computation.27 | convolution fusion | flops 12582912 | bytes 4204544 | tf_op jit(solution)/shard_map/dot_general | solution.py:18
  188.7 16.6 %collective-permute-start.6 = (f32[512]{0:T(512)S(1)}, f32[512]{0:T(512)S(1)}, u32[]{:S(2)}, u32[]{:S(2)}) collective-permute-start(f32[512]{0:T(512)S(1)} %bitcast.26), channel_id=1, source_target_pairs={{0,1},{1,0},{2,3},{3,2},{4,5},{5,4},{6,7},{7,6},{8,9},{9,8},{10,11... | collective-permute-start | bytes 6152 | tf_op jit(solution)/shard_map/ppermute | solution.py:21
  207.3 1.2 collective-permute-done.7
  208.6 2.7 collective-permute-start.8
  212.5 4.7 %fusion.6 = f32[2048,768]{1,0:T(8,128)} fusion(bf16[512,768]{1,0:T(8,128)(2,1)S(1)} %copy-done.3, f32[512]{0:T(512)S(1)} %add_rsqrt_fusion.1, f32[512,2048]{1,0:T(8,128)S(1)} %copy-done.2, f32[2048]{0:T(1024)S(1)} %broadcast_divide_fusion.1, f32[512]{0:T(512)S(1)} %add_divide_fusion), kind=kOutput, calls=%fused_computation.12 | convolution fusion | flops 1614938112 | bytes 11284480 | tf_op jit(solution)/shard_map/dot_general | solution.py:48
  217.3 2.7 convert_reduce_fusion
  220.0 61.0 %psum.31 = f32[2048]{0:T(1024)S(1)} all-reduce(f32[2048]{0:T(1024)S(1)} %convert_reduce_fusion), channel_id=1, replica_groups=mesh['dp'=32,'cent'=8] {'dp'}, use_global_device_ids=true, to_apply=%region_6.0 | all-reduce | flops 2048 | bytes 16384 | tf_op jit(solution)/shard_map/psum | solution.py:51
  281.1 118.6 %all-reduce.2.cloned.1.call-done = f32[2048,768]{1,0:T(8,128)} async-done(((f32[2048,768]{1,0:T(8,128)}), f32[2048,768]{1,0:T(8,128)}) %all-reduce.2.cloned.1.call-update) | async-done | bytes 6291472 | tf_op jit(solution)/shard_map/psum | solution.py:51
  399.7 1.7 dynamic-slice_divide_fusion
  (33 shorter events, 8.5 us)
Async XLA Ops:
  6.5 393.2 %all-reduce.2.cloned.1.call-start = ((), (), s32[]{:S(2)}) async-start(), calls=%async_computation | async-start | bytes 12582912 | tf_op jit(solution)/shard_map/psum | solution.py:51
  14.6 16.1 %copy-start = (f32[512,2048]{1,0:T(8,128)}, f32[512,2048]{1,0:T(8,128)S(1)}, u32[]{:S(2)}) copy-start(f32[512,2048]{1,0:T(8,128)S(1)} %multiply_exponential_fusion) | copy-start | bytes 12582916
  18.2 4.0 collective-permute-start
  22.3 2.4 collective-permute-start.1
  24.7 3.9 collective-permute-start.2
  94.1 29.9 %copy-start.1 = (f32[512,2048]{1,0:T(8,128)S(1)}, f32[512,2048]{1,0:T(8,128)}, u32[]{:S(2)}) copy-start(f32[512,2048]{1,0:T(8,128)} %copy-done) | copy-start | bytes 12582916
  100.1 17.5 %collective-permute-start.3 = (f32[512]{0:T(512)S(1)}, f32[512]{0:T(512)S(1)}, u32[]{:S(2)}, u32[]{:S(2)}) collective-permute-start(f32[512]{0:T(512)S(1)} %bitcast.22), channel_id=1, source_target_pairs={{0,1},{1,0},{2,3},{3,2},{4,5},{5,4},{6,7},{7,6},{8,9},{9,8},{10,11... | collective-permute-start | bytes 6152 | tf_op jit(solution)/shard_map/ppermute | solution.py:21
  117.6 2.4 collective-permute-start.4
  120.0 3.9 collective-permute-start.5
  124.0 88.5 %copy-start.3 = (bf16[512,768]{1,0:T(8,128)(2,1)S(1)}, bf16[512,768]{1,0:T(8,128)(2,1)}, u32[]{:S(2)}) copy-start(bf16[512,768]{1,0:T(8,128)(2,1)} %param.2) | copy-start | bytes 2359300
  182.8 29.7 %copy-start.2 = (f32[512,2048]{1,0:T(8,128)S(1)}, f32[512,2048]{1,0:T(8,128)}, u32[]{:S(2)}) copy-start(f32[512,2048]{1,0:T(8,128)} %copy-done) | copy-start | bytes 12582916
  188.7 17.4 %collective-permute-start.6 = (f32[512]{0:T(512)S(1)}, f32[512]{0:T(512)S(1)}, u32[]{:S(2)}, u32[]{:S(2)}) collective-permute-start(f32[512]{0:T(512)S(1)} %bitcast.26), channel_id=1, source_target_pairs={{0,1},{1,0},{2,3},{3,2},{4,5},{5,4},{6,7},{7,6},{8,9},{9,8},{10,11... | collective-permute-start | bytes 6152 | tf_op jit(solution)/shard_map/ppermute | solution.py:21
  206.1 2.4 collective-permute-start.7
  208.6 3.9 collective-permute-start.8
Sparse Core Ops, SparseCore 0:
  217.4 182.2 all-reduce.1
